TPU v7x, 32 devices: a whole 2x2x4 slice. The times are simulated.
32 devices in a mesh: grp: 2 (over x), pool: 16 (over z, y, core).
Axes of the slice: x: 2, y: 2, z: 4, core: 2. Of those that a mesh axis runs over, the one named last changes fastest.
Arguments:
- queries: bfloat16 [32, 128, 1024], P(('grp', 'pool')), parts along dimension 0, may hold values from -400 to 400
- new_kv: bfloat16 [32, 128, 256], P(('grp', 'pool')), parts along dimension 0, may hold values from -16 to 16
- pool_kv: bfloat16 [64, 8, 128, 256], P(('grp', 'pool')), parts along dimension 0, may hold values from -16 to 16
- hit_slots: int32 [4, 16], P('grp'), parts along dimension 0, may hold values from 0 to 31, as said below
- prefix_blocks: int32 [4], P('grp'), parts along dimension 0, may hold values from 1 to 16, 20 in all
- new_owners: int32 [4, 2], P('grp'), parts along dimension 0, may hold values from 0 to 15, as said below
Outputs:
- attended: bfloat16 [32, 128, 1024], P(('grp', 'pool')), parts along dimension 0
- new_store: bfloat16 [32, 8, 128, 256], P(('grp', 'pool')), parts along dimension 0
There are 2 independent parts, one for each index of `grp`. A program takes and returns all parts, laid end to end along the dimension named above; each array names one. Nothing has to cross between parts.
Inputs may be any that keep to these rules, and one draw needn't show every extreme that they name: `hit_slots`: slot s lies on owner s // 2. Block j of request r lies on owner (f + j) mod 16, where f depends on r and is a multiple of 4; one owner keeps different requests in different slots. Entries with j >= prefix_blocks[r] are unused. `prefix_blocks`: they sum to 20. `new_owners`: all 4 entries are distinct.
All inputs are finite; a program needn't handle non-finite values.
Results may differ from a plain program's by a relative error of at most 0.009.
Values may be sent and summed in bfloat16 or wider, within the bound.
No kernel may reach another device: no remote copies, remote signals or barrier semaphores. Data moves between devices by JAX's collectives and lax.ppermute only.
A program may use at most 64 MiB of HBM per device.

v0:
```python
import math
import jax
import jax.numpy as jnp
from jax import lax
from jax.sharding import PartitionSpec as P

group_slots = 4
minus_big = -1e30


def fold_keys(state_now, query_rows, key_rows, values, usable, score_scale):
    maximum, totals, accumulated = state_now
    scores = (
        jnp.einsum("tgd,kd->tgk", query_rows, key_rows, preferred_element_type=jnp.float32)
        * score_scale
    )
    scores = jnp.where(usable, scores, minus_big)
    maximum_new = jnp.maximum(maximum, jnp.max(scores, axis=2))
    weights = jnp.where(usable, jnp.exp(scores - maximum_new[:, :, None]), 0.0)
    factor = jnp.exp(maximum - maximum_new)
    totals = totals * factor + jnp.sum(weights, axis=2)
    accumulated = accumulated * factor[:, :, None] + jnp.einsum(
        "tgk,kd->tgd", weights.astype(jnp.bfloat16), values, preferred_element_type=jnp.float32
    )
    return (maximum_new, totals, accumulated)


def attend_blocks(state_now, query_rows, stored, first_slot, live_count, score_scale):
    slot_total = stored.shape[0]
    block_len = stored.shape[1]
    row_width = stored.shape[2]
    head_dim = row_width // 2
    loop_steps = (live_count + group_slots - 1) // group_slots
    offsets = jnp.arange(group_slots * block_len, dtype=jnp.int32) // block_len

    def advance(turn_index, state_in):
        start_slot = (first_slot + turn_index * group_slots) % slot_total
        block_rows = lax.dynamic_slice_in_dim(stored, start_slot, group_slots, 0).reshape(
            group_slots * block_len, row_width
        )
        usable = (turn_index * group_slots + offsets < live_count)[None, None, :]
        return fold_keys(
            state_in,
            query_rows,
            block_rows[:, :head_dim],
            block_rows[:, head_dim:],
            usable,
            score_scale,
        )

    return lax.fori_loop(0, loop_steps, advance, state_now)


def on_device(queries, new_kv, pool_kv, hit_slots, prefix_blocks, new_owners):
    my_index = lax.axis_index("pool")
    slot_count = pool_kv.shape[0]
    kv_heads = pool_kv.shape[1]
    block_len = pool_kv.shape[2]
    row_width = pool_kv.shape[3]
    head_dim = row_width // 2
    requests = hit_slots.shape[0]
    longest = hit_slots.shape[1]
    groups = queries.shape[2] // head_dim
    score_scale = 1.0 / math.sqrt(head_dim)
    request = my_index // kv_heads
    positions = jnp.arange(longest, dtype=jnp.int32)
    is_live = positions[None, :] < prefix_blocks[:, None]
    on_me = (hit_slots // slot_count == my_index) & is_live
    holds_block = jnp.any(on_me, axis=1)
    local_slot = jnp.sum(jnp.where(on_me, hit_slots % slot_count, 0), axis=1)
    picked = jnp.take(pool_kv, local_slot, axis=0)
    outgoing = jnp.where(holds_block[:, None, None, None], picked, jnp.zeros_like(picked))
    outgoing = outgoing.reshape(requests * kv_heads, block_len, row_width)
    fetched = lax.all_to_all(outgoing, "pool", split_axis=0, concat_axis=0, tiled=True)
    query_rows = queries[0].reshape(block_len, groups, head_dim)
    own_new = new_kv[0]
    causal = (jnp.arange(block_len)[None, :] <= jnp.arange(block_len)[:, None])[:, None, :]
    empty_state = (
        jnp.full((block_len, groups), minus_big, jnp.float32),
        jnp.zeros((block_len, groups), jnp.float32),
        jnp.zeros((block_len, groups, head_dim), jnp.float32),
    )
    state_now = fold_keys(
        empty_state, query_rows, own_new[:, :head_dim], own_new[:, head_dim:], causal, score_scale
    )
    own_length = prefix_blocks[request]
    own_first = hit_slots[request, 0] // slot_count
    state_now = attend_blocks(state_now, query_rows, fetched, own_first, own_length, score_scale)
    attended = (
        (state_now[2] / state_now[1][:, :, None])
        .reshape(block_len, groups * head_dim)
        .astype(jnp.bfloat16)[None]
    )
    arrived = lax.all_gather(new_kv, "pool", axis=0, tiled=True)
    owned_by_me = jnp.any(new_owners == my_index, axis=1)
    source_request = jnp.sum(jnp.where(owned_by_me, jnp.arange(requests, dtype=jnp.int32), 0))
    owned = jnp.any(owned_by_me)
    new_block = lax.dynamic_slice_in_dim(arrived, source_request * kv_heads, kv_heads, 0)
    new_store = jnp.where(owned, new_block, jnp.zeros_like(new_block))[None]
    return (attended, new_store)


def solution(mesh):
    placed = (
        P(("grp", "pool"), None, None),
        P(("grp", "pool"), None, None),
        P(("grp", "pool"), None, None, None),
        P("grp", None),
        P("grp"),
        P("grp", None),
    )
    return jax.shard_map(
        on_device,
        mesh=mesh,
        in_specs=placed,
        out_specs=(P(("grp", "pool"), None, None), P(("grp", "pool"), None, None, None)),
        check_vma=False,
    )
```

profile of v0, /device:TPU:0, one launch (start us, length us, event | category | flops | bytes accessed | tf_op | source)
XLA Modules:
  0.0 74.9 jit_solution(3903400085508740048)
XLA Ops:
  7.2 0.0 copy-start
  7.2 1.0 %fusion.36 = (pred[2]{0:T(512)(128)(4,1)S(1)}, pred[2,16]{1,0:T(4,128)(4,1)S(1)}) fusion(s32[2]{0:T(128)} %param.12, s32[]{:T(128)S(6)} %axis_index.12, s32[2,16]{1,0:T(2,128)} %param.11), kind=kLoop, calls=%fused_computation.73 | loop fusion | flops 606 | bytes 174 | tf_op jit(solution)/shard_map/reduce_or | solution.py:69
  8.2 0.8 %fusion.30 = s32[2]{0:T(128)S(1)} fusion(pred[2,16]{1,0:T(4,128)(4,1)S(1)} %get-tuple-element.196, s32[2,16]{1,0:T(2,128)} %param.11), kind=kLoop, calls=%fused_computation.62 | loop fusion | flops 414 | bytes 168 | tf_op jit(solution)/shard_map/reduce_sum | solution.py:70
  9.0 0.1 broadcast_in_dim.117
  9.1 0.1 broadcast_in_dim.118
  9.1 0.1 broadcast_in_dim.114
  9.2 0.1 broadcast_in_dim.115
  9.3 0.0 copy-done
  9.3 0.6 gather_fusion
  9.9 0.0 copy-start.3
  9.9 0.0 copy-start.5
  10.0 0.0 copy-start.2
  10.0 1.3 %fusion.22 = bf16[16,128,256]{2,1,0:T(8,128)(2,1)} fusion(bf16[2,8,128,256]{3,2,1,0:T(8,128)(2,1)S(1)} %gather_fusion, pred[16]{0:T(512)(128)(4,1)S(1)} %broadcast_in_dim.118, pred[16]{0:T(512)(128)(4,1)S(1)} %broadcast_in_dim.115), kind=kLoop, calls=%fused_computation.37 | loop fusion | flops 1048576 | bytes 2097184 | tf_op jit(solution)/shard_map/jit(_where)/select_n | solution.py:72
  11.3 0.0 copy-start.4
  11.3 0.0 copy-start.1
  11.3 7.5 %all-to-all-start = ((bf16[16,128,256]{2,1,0:T(8,128)(2,1)}), bf16[16,128,256]{2,1,0:T(8,128)(2,1)S(1)}, u32[]{:S(2)}, u32[]{:S(2)}) async-start(bf16[16,128,256]{2,1,0:T(8,128)(2,1)} %fusion.22), calls=%async_computation | async-start | bytes 2097152 | tf_op jit(solution)/shard_map/all_to_all | solution.py:74
  18.8 0.0 all-gather.2.cloned.1.call-start
  18.9 0.7 all-gather.2.cloned.1.call-update
  19.6 0.0 copy-done.3
  19.6 0.5 constant_dynamic-slice_fusion.1
  22.7 0.0 copy-done.5
  22.7 0.6 dynamic_slice.15
  24.0 0.0 copy-done.2
  24.0 0.2 copy.18
  24.2 0.2 copy.21
  24.4 0.0 copy-done.4
  24.4 0.7 fusion.34
  25.0 0.7 select_reduce_fusion
  26.4 0.0 copy-done.1
  26.4 0.2 fusion.37
  26.6 0.1 fusion.24
  26.7 0.3 convolution_add_fusion.1
  27.1 15.8 %all-to-all-done = bf16[16,128,256]{2,1,0:T(8,128)(2,1)S(1)} async-done(((bf16[16,128,256]{2,1,0:T(8,128)(2,1)}), bf16[16,128,256]{2,1,0:T(8,128)(2,1)S(1)}, u32[]{:S(2)}, u32[]{:S(2)}) %all-to-all-start) | async-done | bytes 1048608 | tf_op jit(solution)/shard_map/all_to_all | solution.py:74
  42.8 2.8 %while.17 = (s32[]{:T(128)}, f32[128,8]{0,1:T(8,128)S(1)}, f32[128,8]{0,1:T(8,128)S(1)}, f32[128,8,128]{2,0,1:T(8,128)S(1)}, s32[]{:T(128)}, /*index=5*/s32[]{:T...) while((s32[]{:T(128)}, f32[128,8]{0,1:T(8,128)S(1)}, ...), condition=%wide.region_7.8_spmd.clone, body=%wide.region_4.7_spmd.clone.sunk | while | flops 275520512 | bytes 8457016 | solution.py:51
  42.8 0.7 fusion.46
  43.5 0.5 bitcast_reduce_fusion.2
  44.0 0.6 fusion.47
  44.6 1.0 %convolution_add_fusion.3 = f32[128,8,128]{2,0,1:T(8,128)S(1)} fusion(f32[512,128,8]{1,0,2:T(8,128)S(1)} %get-tuple-element.264, f32[128,8]{0,1:T(8,128)S(1)} %max.8, pred[512]{0:T(512)(128)(4,1)S(1)} %fusion.46, f32[128,8,128]{2,0,1:T(8,128)S(1)} %get-tuple-element.284, f32[128,8]{0,1:T(8,128)S(1)} %get-tuple-element.266, ...), kind=kOutput, calls=%fused_computation.9.clone.1 | convolution fusion | flops 137101312 | bytes 3286016 | tf_op jit(solution)/shard_map/while/body/tgk,kd->tgd/dot_general | solution.py:22
  45.6 0.2 divide_convert_fusion
  45.9 0.2 copy.22
  46.0 0.8 %convert_element_type.24 = bf16[1,128,1024]{2,1,0:T(8,128)(2,1)} reshape(bf16[128,8,128]{2,1,0:T(8,128)(2,1)S(1)} %copy.22) | data formatting | bytes 524288 | tf_op jit(solution)/shard_map/convert_element_type | solution.py:92
  46.9 18.7 %all-gather.2.cloned.1.call-done = bf16[16,128,256]{2,1,0:T(8,128)(2,1)} async-done(((bf16[1,128,256]{2,1,0:T(8,128)(2,1)}), bf16[16,128,256]{2,1,0:T(8,128)(2,1)}) %all-gather.2.cloned.1.call-update) | async-done | bytes 1048592 | tf_op jit(solution)/shard_map/all_gather | solution.py:94
  65.6 2.5 %select_bitcast_fusion = bf16[1,8,128,256]{3,2,1,0:T(8,128)(2,1)} fusion(bf16[16,128,256]{2,1,0:T(8,128)(2,1)} %all-gather.2.cloned.1.call-done, s32[]{:T(128)S(6)} %select_n.133, pred[]{:T(512)} %get-tuple-element.173), kind=kLoop, calls=%fused_computation.38 | loop fusion | flops 262144 | bytes 1048581 | tf_op jit(solution)/shard_map/broadcast_in_dim | solution.py:99
  (10 shorter events, 0.1 us)
Async XLA Ops:
  7.2 2.1 %copy-start = (bf16[2,8,128,256]{3,2,1,0:T(8,128)(2,1)S(1)}, bf16[2,8,128,256]{3,2,1,0:T(8,128)(2,1)}, u32[]{:S(2)}) copy-start(bf16[2,8,128,256]{3,2,1,0:T(8,128)(2,1)} %param.10) | copy-start | bytes 3145732
  9.9 9.6 %copy-start.3 = (s32[2,16]{1,0:T(2,128)S(1)}, s32[2,16]{1,0:T(2,128)}, u32[]{:S(2)}) copy-start(s32[2,16]{1,0:T(2,128)} %param.11) | copy-start | bytes 388
  9.9 12.8 %copy-start.5 = (s32[2]{0:T(128)S(1)}, s32[2]{0:T(128)}, u32[]{:S(2)}) copy-start(s32[2]{0:T(128)} %param.12) | copy-start | bytes 28
  10.0 14.0 %copy-start.2 = (bf16[1,128,1024]{2,1,0:T(8,128)(2,1)S(1)}, bf16[1,128,1024]{2,1,0:T(8,128)(2,1)}, u32[]{:S(2)}) copy-start(bf16[1,128,1024]{2,1,0:T(8,128)(2,1)} %param.8) | copy-start | bytes 786436
  11.3 13.1 %copy-start.4 = (s32[2,2]{1,0:T(2,128)S(1)}, s32[2,2]{1,0:T(2,128)}, u32[]{:S(2)}) copy-start(s32[2,2]{1,0:T(2,128)} %param.13) | copy-start | bytes 52
  11.3 15.1 %copy-start.1 = (bf16[1,128,256]{2,1,0:T(8,128)(2,1)S(1)}, bf16[1,128,256]{2,1,0:T(8,128)(2,1)}, u32[]{:S(2)}) copy-start(bf16[1,128,256]{2,1,0:T(8,128)(2,1)} %param.9) | copy-start | bytes 196612
  11.3 31.6 %all-to-all-start = ((bf16[16,128,256]{2,1,0:T(8,128)(2,1)}), bf16[16,128,256]{2,1,0:T(8,128)(2,1)S(1)}, u32[]{:S(2)}, u32[]{:S(2)}) async-start(bf16[16,128,256]{2,1,0:T(8,128)(2,1)} %fusion.22), calls=%async_computation | async-start | bytes 2097152 | tf_op jit(solution)/shard_map/all_to_all | solution.py:74
  18.8 46.8 %all-gather.2.cloned.1.call-start = ((), (), s32[]{:S(2)}) async-start(), calls=%async_computation.1 | async-start | bytes 1114112 | tf_op jit(solution)/shard_map/all_gather | solution.py:94
Sparse Core Ops, SparseCore 0:
  21.8 43.7 all-gather.1
where the time goes:
time: 75.3 us; the launch traced here: 74.9 us
  waiting for transfers between devices  35.1 us (47%)
  between operations  18.1 us (24%)
  other arithmetic  8.52 us (11%)
  starting transfers between devices  7.59 us (10%)
  local copies, waits for them, and re-layouts  3.44 us (5%)
  matrix products  2.02 us (3%)
    all_gather x1, waiting for transfers between devices, on_device(): arrived = lax.all_gather(new_kv, 'pool', axis=0, tiled=True)  18.7 us
    all_to_all x1, waiting for transfers between devices, on_device(): lax.all_to_all(outgoing, 'pool', split_axis=0, concat_axis=0, tiled=True)  15.8 us
    all_to_all x1, starting transfers between devices, on_device(): lax.all_to_all(outgoing, 'pool', split_axis=0, concat_axis=0, tiled=True)  7.55 us
    broadcast_in_dim x1, other arithmetic, on_device(): new_store = jnp.where(owned, new_block, jnp.zeros_like(new_block))[None]  2.49 us
  transfers between devices with their start and end apart: 2, of which 2 were waited for; matrix products, arithmetic and copies ran while one was open for 10% of the time, Pallas kernels for 0%

commit v1 on v0

--- a/solution.py
+++ b/solution.py
@@ -1,3 +1,4 @@
+import functools
 import math
 import jax
 import jax.numpy as jnp
@@ -6,6 +7,26 @@
 
 group_slots = 4
 minus_big = -1e30
+
+
+def take_fields_in(m, net_axis):
+    num = lax.psum(1, net_axis)
+    pieces_in = []
+    for j0 in tuple(range(num)):
+        pieces_in.append((j0, (j0 + 1) % num))
+
+    def values_number(before):
+        if len(before) == num:
+            return before
+        t_next = values_number([lax.ppermute(before[0], net_axis, pieces_in), *before])
+        return t_next
+
+    reached = jnp.concatenate(values_number([m]), 0)
+    n_now = jnp.roll(reached, (lax.axis_index(net_axis) + 1) * m.shape[0], axis=0)
+    return n_now
+
+
+_carry_ladders = functools.partial(take_fields_in, net_axis="pool")
 
 
 def fold_keys(state_now, query_rows, key_rows, values, usable, score_scale):
@@ -91,7 +112,7 @@
         .reshape(block_len, groups * head_dim)
         .astype(jnp.bfloat16)[None]
     )
-    arrived = lax.all_gather(new_kv, "pool", axis=0, tiled=True)
+    arrived = _carry_ladders(new_kv)
     owned_by_me = jnp.any(new_owners == my_index, axis=1)
     source_request = jnp.sum(jnp.where(owned_by_me, jnp.arange(requests, dtype=jnp.int32), 0))
     owned = jnp.any(owned_by_me)

time: 75.3 us -> 142 us (1.89)
  the two profiles are of different devices: /device:TPU:0 before, /device:TPU:31 now
where the time goes in v1:
time: 142 us; the launch traced here: 141 us
  starting transfers between devices  72.3 us (51%)
  waiting for transfers between devices  31 us (22%)
  local copies, waits for them, and re-layouts  15.6 us (11%)
  other arithmetic  10.8 us (8%)
  matrix products  6.35 us (4%)
  between operations  4.63 us (3%)
    ppermute x15, starting transfers between devices, values_number(): lax.ppermute(before[0], net_axis, pieces_in)  66.5 us
    ppermute x15, waiting for transfers between devices, values_number(): lax.ppermute(before[0], net_axis, pieces_in)  31 us
    unnamed x69, local copies, waits for them, and re-layouts  12.4 us
    all_to_all x1, starting transfers between devices, on_device(): lax.all_to_all(outgoing, 'pool', split_axis=0, concat_axis=0, tiled=True)  5.87 us
    dot_general x5, matrix products, fold_keys(): jnp.einsum('tgk,kd->tgd', weights.astype(jnp.bfloat16), values, preferred...  4.3 us
  transfers between devices with their start and end apart: 16, of which 13 were waited for; matrix products, arithmetic and copies ran while one was open for 15% of the time, Pallas kernels for 0%

profile of v1, /device:TPU:31, one launch (start us, length us, event | category | flops | bytes accessed | tf_op | source)
XLA Modules:
  0.0 141.1 jit_solution(3429211989464040780)
XLA Ops:
  0.6 0.5 collective-permute-start
  1.1 1.6 %collective-permute-done = bf16[1,128,256]{2,1,0:T(8,128)(2,1)S(1)} collective-permute-done((bf16[1,128,256]{2,1,0:T(8,128)(2,1)}, bf16[1,128,256]{2,1,0:T(8,128)(2,1)S(1)}, u32[]{:S(2)}, u32[]{:S(2)}) %collective-permute-start) | collective-permute-done | bytes 65568 | tf_op jit(solution)/shard_map/ppermute | solution.py:21
  2.8 5.0 %collective-permute-start.1 = (bf16[1,128,256]{2,1,0:T(8,128)(2,1)S(1)}, bf16[1,128,256]{2,1,0:T(8,128)(2,1)S(1)}, u32[]{:S(2)}, u32[]{:S(2)}) collective-permute-start(bf16[1,128,256]{2,1,0:T(8,128)(2,1)S(1)} %collective-permute-done), channel_id=1, source_target_pairs={{0,1},{1,2},{2,3},{3,4},{4,5},{5,6},{6,7},{7,8},{8,9},{9,10},{10,1... | collective-permute-start | bytes 196616 | tf_op jit(solution)/shard_map/ppermute | solution.py:21
  7.7 0.9 fusion.36
  9.1 5.1 %collective-permute-start.2 = (bf16[1,128,256]{2,1,0:T(8,128)(2,1)S(1)}, bf16[1,128,256]{2,1,0:T(8,128)(2,1)S(1)}, u32[]{:S(2)}, u32[]{:S(2)}) collective-permute-start(bf16[1,128,256]{2,1,0:T(8,128)(2,1)S(1)} %collective-permute-done.1), channel_id=1, source_target_pairs={{0,1},{1,2},{2,3},{3,4},{4,5},{5,6},{6,7},{7,8},{8,9},{9,10},{10,1... | collective-permute-start | bytes 196616 | tf_op jit(solution)/shard_map/ppermute | solution.py:21
  14.1 0.8 fusion.30
  14.9 0.5 collective-permute-done.2
  15.5 5.1 %collective-permute-start.3 = (bf16[1,128,256]{2,1,0:T(8,128)(2,1)S(1)}, bf16[1,128,256]{2,1,0:T(8,128)(2,1)S(1)}, u32[]{:S(2)}, u32[]{:S(2)}) collective-permute-start(bf16[1,128,256]{2,1,0:T(8,128)(2,1)S(1)} %collective-permute-done.2), channel_id=1, source_target_pairs={{0,1},{1,2},{2,3},{3,4},{4,5},{5,6},{6,7},{7,8},{8,9},{9,10},{10,1... | collective-permute-start | bytes 196616 | tf_op jit(solution)/shard_map/ppermute | solution.py:21
  20.5 1.3 collective-permute-done.3
  21.9 5.1 %collective-permute-start.4 = (bf16[1,128,256]{2,1,0:T(8,128)(2,1)S(1)}, bf16[1,128,256]{2,1,0:T(8,128)(2,1)S(1)}, u32[]{:S(2)}, u32[]{:S(2)}) collective-permute-start(bf16[1,128,256]{2,1,0:T(8,128)(2,1)S(1)} %collective-permute-done.3), channel_id=1, source_target_pairs={{0,1},{1,2},{2,3},{3,4},{4,5},{5,6},{6,7},{7,8},{8,9},{9,10},{10,1... | collective-permute-start | bytes 196616 | tf_op jit(solution)/shard_map/ppermute | solution.py:21
  27.2 1.0 collective-permute-done.4
  28.2 5.1 %collective-permute-start.5 = (bf16[1,128,256]{2,1,0:T(8,128)(2,1)S(1)}, bf16[1,128,256]{2,1,0:T(8,128)(2,1)S(1)}, u32[]{:S(2)}, u32[]{:S(2)}) collective-permute-start(bf16[1,128,256]{2,1,0:T(8,128)(2,1)S(1)} %collective-permute-done.4), channel_id=1, source_target_pairs={{0,1},{1,2},{2,3},{3,4},{4,5},{5,6},{6,7},{7,8},{8,9},{9,10},{10,1... | collective-permute-start | bytes 196616 | tf_op jit(solution)/shard_map/ppermute | solution.py:21
  33.3 0.6 gather_fusion
  34.0 0.7 collective-permute-done.5
  34.6 5.1 %collective-permute-start.6 = (bf16[1,128,256]{2,1,0:T(8,128)(2,1)S(1)}, bf16[1,128,256]{2,1,0:T(8,128)(2,1)S(1)}, u32[]{:S(2)}, u32[]{:S(2)}) collective-permute-start(bf16[1,128,256]{2,1,0:T(8,128)(2,1)S(1)} %collective-permute-done.5), channel_id=1, source_target_pairs={{0,1},{1,2},{2,3},{3,4},{4,5},{5,6},{6,7},{7,8},{8,9},{9,10},{10,1... | collective-permute-start | bytes 196616 | tf_op jit(solution)/shard_map/ppermute | solution.py:21
  39.7 1.2 fusion.22
  40.9 5.9 %all-to-all-start = ((bf16[16,128,256]{2,1,0:T(8,128)(2,1)}), bf16[16,128,256]{2,1,0:T(8,128)(2,1)S(1)}, u32[]{:S(2)}, u32[]{:S(2)}) async-start(bf16[16,128,256]{2,1,0:T(8,128)(2,1)} %fusion.22), calls=%async_computation | async-start | bytes 2097152 | tf_op jit(solution)/shard_map/all_to_all | solution.py:95
  47.2 18.2 %collective-permute-done.7 = bf16[1,128,256]{2,1,0:T(8,128)(2,1)S(1)} collective-permute-done((bf16[1,128,256]{2,1,0:T(8,128)(2,1)S(1)}, bf16[1,128,256]{2,1,0:T(8,128)(2,1)S(1)}, u32[]{:S(2)}, u32[]{:S(2)}) %collective-permute-start.7) | collective-permute-done | bytes 65568 | tf_op jit(solution)/shard_map/ppermute | solution.py:21
  65.3 5.1 %collective-permute-start.8 = (bf16[1,128,256]{2,1,0:T(8,128)(2,1)S(1)}, bf16[1,128,256]{2,1,0:T(8,128)(2,1)S(1)}, u32[]{:S(2)}, u32[]{:S(2)}) collective-permute-start(bf16[1,128,256]{2,1,0:T(8,128)(2,1)S(1)} %collective-permute-done.7), channel_id=1, source_target_pairs={{0,1},{1,2},{2,3},{3,4},{4,5},{5,6},{6,7},{7,8},{8,9},{9,10},{10,1... | collective-permute-start | bytes 196616 | tf_op jit(solution)/shard_map/ppermute | solution.py:21
  70.7 1.1 collective-permute-done.8
  71.8 5.1 %collective-permute-start.9 = (bf16[1,128,256]{2,1,0:T(8,128)(2,1)S(1)}, bf16[1,128,256]{2,1,0:T(8,128)(2,1)S(1)}, u32[]{:S(2)}, u32[]{:S(2)}) collective-permute-start(bf16[1,128,256]{2,1,0:T(8,128)(2,1)S(1)} %collective-permute-done.8), channel_id=1, source_target_pairs={{0,1},{1,2},{2,3},{3,4},{4,5},{5,6},{6,7},{7,8},{8,9},{9,10},{10,1... | collective-permute-start | bytes 196616 | tf_op jit(solution)/shard_map/ppermute | solution.py:21
  76.9 1.3 collective-permute-done.9
  78.2 5.1 %collective-permute-start.10 = (bf16[1,128,256]{2,1,0:T(8,128)(2,1)S(1)}, bf16[1,128,256]{2,1,0:T(8,128)(2,1)S(1)}, u32[]{:S(2)}, u32[]{:S(2)}) collective-permute-start(bf16[1,128,256]{2,1,0:T(8,128)(2,1)S(1)} %collective-permute-done.9), channel_id=1, source_target_pairs={{0,1},{1,2},{2,3},{3,4},{4,5},{5,6},{6,7},{7,8},{8,9},{9,10},{10,1... | collective-permute-start | bytes 196616 | tf_op jit(solution)/shard_map/ppermute | solution.py:21
  83.4 1.2 collective-permute-done.10
  84.6 5.1 %collective-permute-start.11 = (bf16[1,128,256]{2,1,0:T(8,128)(2,1)S(1)}, bf16[1,128,256]{2,1,0:T(8,128)(2,1)}, u32[]{:S(2)}, u32[]{:S(2)}) collective-permute-start(bf16[1,128,256]{2,1,0:T(8,128)(2,1)S(1)} %collective-permute-done.10), channel_id=1, source_target_pairs={{0,1},{1,2},{2,3},{3,4},{4,5},{5,6},{6,7},{7,8},{8,9},{9,10},{10,1... | collective-permute-start | bytes 196616 | tf_op jit(solution)/shard_map/ppermute | solution.py:21
  89.7 1.3 collective-permute-done.11
  91.0 5.2 %collective-permute-start.12 = (bf16[1,128,256]{2,1,0:T(8,128)(2,1)}, bf16[1,128,256]{2,1,0:T(8,128)(2,1)}, u32[]{:S(2)}, u32[]{:S(2)}) collective-permute-start(bf16[1,128,256]{2,1,0:T(8,128)(2,1)} %collective-permute-done.11), channel_id=1, source_target_pairs={{0,1},{1,2},{2,3},{3,4},{4,5},{5,6},{6,7},{7,8},{8,9},{9,10},{10,1... | collective-permute-start | bytes 196616 | tf_op jit(solution)/shard_map/ppermute | solution.py:21
  96.5 1.3 collective-permute-done.12
  97.8 5.1 %collective-permute-start.13 = (bf16[1,128,256]{2,1,0:T(8,128)(2,1)}, bf16[1,128,256]{2,1,0:T(8,128)(2,1)}, u32[]{:S(2)}, u32[]{:S(2)}) collective-permute-start(bf16[1,128,256]{2,1,0:T(8,128)(2,1)} %collective-permute-done.12), channel_id=1, source_target_pairs={{0,1},{1,2},{2,3},{3,4},{4,5},{5,6},{6,7},{7,8},{8,9},{9,10},{10,1... | collective-permute-start | bytes 196616 | tf_op jit(solution)/shard_map/ppermute | solution.py:21
  102.9 0.7 fusion.34
  103.6 0.9 collective-permute-done.13
  104.5 5.1 %collective-permute-start.14 = (bf16[1,128,256]{2,1,0:T(8,128)(2,1)}, bf16[1,128,256]{2,1,0:T(8,128)(2,1)}, u32[]{:S(2)}, u32[]{:S(2)}) collective-permute-start(bf16[1,128,256]{2,1,0:T(8,128)(2,1)} %collective-permute-done.13), channel_id=1, source_target_pairs={{0,1},{1,2},{2,3},{3,4},{4,5},{5,6},{6,7},{7,8},{8,9},{9,10},{10,1... | collective-permute-start | bytes 196616 | tf_op jit(solution)/shard_map/ppermute | solution.py:21
  109.6 0.6 select_reduce_fusion
  110.8 0.5 constant_dynamic-slice_fusion.1
  113.7 0.6 dynamic_slice.20
  115.2 0.9 constant_dynamic-update-slice_fusion.31
  116.1 0.8 constant_dynamic-update-slice_fusion.30
  117.0 0.8 constant_dynamic-update-slice_fusion.29
  117.8 0.8 constant_dynamic-update-slice_fusion.28
  118.6 0.8 constant_dynamic-update-slice_fusion.27
  119.5 0.8 constant_dynamic-update-slice_fusion.26
  120.3 0.8 constant_dynamic-update-slice_fusion.25
  121.2 0.8 constant_dynamic-update-slice_fusion.24
  122.0 0.8 constant_dynamic-update-slice_fusion.23
  122.9 0.8 constant_dynamic-update-slice_fusion.22
  123.8 0.8 constant_dynamic-update-slice_fusion.15
  124.6 0.8 constant_dynamic-update-slice_fusion.14
  125.5 0.8 constant_dynamic-update-slice_fusion.13
  126.3 0.8 constant_dynamic-update-slice_fusion.12
  127.4 1.5 %select_bitcast_fusion = bf16[1,8,128,256]{3,2,1,0:T(8,128)(2,1)} fusion(bf16[32,128,256]{2,1,0:T(8,128)(2,1)S(1)} %constant_dynamic-update-slice_fusion, s32[]{:T(128)S(6)} %dynamic_slice.22, pred[]{:T(512)} %get-tuple-element.164), kind=kLoop, calls=%fused_computation.38 | loop fusion | flops 262144 | bytes 1048581 | tf_op jit(solution)/shard_map/broadcast_in_dim | solution.py:120
  128.8 11.0 %while.17 = (s32[]{:T(128)}, f32[128,8]{0,1:T(8,128)S(1)}, f32[128,8]{0,1:T(8,128)S(1)}, f32[128,8,128]{2,0,1:T(8,128)S(1)}, s32[]{:T(128)}, /*index=5*/s32[]{:T...) while((s32[]{:T(128)}, f32[128,8]{0,1:T(8,128)S(1)}, ...), condition=%wide.region_7.8_spmd.clone, body=%wide.region_4.7_spmd.clone.sunk | while | flops 275520512 | bytes 8457016 | solution.py:72
  128.9 0.6 fusion.46
  129.9 0.6 fusion.47
  130.6 1.0 convolution_add_fusion.3
  131.6 0.6 fusion.46
  132.7 0.6 fusion.47
  133.3 1.0 convolution_add_fusion.3
  134.4 0.6 fusion.46
  135.5 0.6 fusion.47
  136.1 1.0 convolution_add_fusion.3
  137.2 0.6 fusion.46
  138.2 0.6 fusion.47
  138.9 1.0 convolution_add_fusion.3
  140.3 0.8 convert_element_type.24
  (96 shorter events, 4.5 us)
Async XLA Ops:
  0.6 32.7 %copy-start = (bf16[2,8,128,256]{3,2,1,0:T(8,128)(2,1)S(1)}, bf16[2,8,128,256]{3,2,1,0:T(8,128)(2,1)}, u32[]{:S(2)}) copy-start(bf16[2,8,128,256]{3,2,1,0:T(8,128)(2,1)} %param.10) | copy-start | bytes 3145732
  0.6 2.1 %collective-permute-start = (bf16[1,128,256]{2,1,0:T(8,128)(2,1)}, bf16[1,128,256]{2,1,0:T(8,128)(2,1)S(1)}, u32[]{:S(2)}, u32[]{:S(2)}) collective-permute-start(bf16[1,128,256]{2,1,0:T(8,128)(2,1)} %param.9), channel_id=1, source_target_pairs={{0,1},{1,2},{2,3},{3,4},{4,5},{5,6},{6,7},{7,8},{8,9},{9,10},{10,1... | collective-permute-start | bytes 196616 | tf_op jit(solution)/shard_map/ppermute | solution.py:21
  2.8 6.3 %collective-permute-start.1 = (bf16[1,128,256]{2,1,0:T(8,128)(2,1)S(1)}, bf16[1,128,256]{2,1,0:T(8,128)(2,1)S(1)}, u32[]{:S(2)}, u32[]{:S(2)}) collective-permute-start(bf16[1,128,256]{2,1,0:T(8,128)(2,1)S(1)} %collective-permute-done), channel_id=1, source_target_pairs={{0,1},{1,2},{2,3},{3,4},{4,5},{5,6},{6,7},{7,8},{8,9},{9,10},{10,1... | collective-permute-start | bytes 196616 | tf_op jit(solution)/shard_map/ppermute | solution.py:21
  9.1 6.4 %collective-permute-start.2 = (bf16[1,128,256]{2,1,0:T(8,128)(2,1)S(1)}, bf16[1,128,256]{2,1,0:T(8,128)(2,1)S(1)}, u32[]{:S(2)}, u32[]{:S(2)}) collective-permute-start(bf16[1,128,256]{2,1,0:T(8,128)(2,1)S(1)} %collective-permute-done.1), channel_id=1, source_target_pairs={{0,1},{1,2},{2,3},{3,4},{4,5},{5,6},{6,7},{7,8},{8,9},{9,10},{10,1... | collective-permute-start | bytes 196616 | tf_op jit(solution)/shard_map/ppermute | solution.py:21
  15.5 6.4 %collective-permute-start.3 = (bf16[1,128,256]{2,1,0:T(8,128)(2,1)S(1)}, bf16[1,128,256]{2,1,0:T(8,128)(2,1)S(1)}, u32[]{:S(2)}, u32[]{:S(2)}) collective-permute-start(bf16[1,128,256]{2,1,0:T(8,128)(2,1)S(1)} %collective-permute-done.2), channel_id=1, source_target_pairs={{0,1},{1,2},{2,3},{3,4},{4,5},{5,6},{6,7},{7,8},{8,9},{9,10},{10,1... | collective-permute-start | bytes 196616 | tf_op jit(solution)/shard_map/ppermute | solution.py:21
  21.9 6.4 %collective-permute-start.4 = (bf16[1,128,256]{2,1,0:T(8,128)(2,1)S(1)}, bf16[1,128,256]{2,1,0:T(8,128)(2,1)S(1)}, u32[]{:S(2)}, u32[]{:S(2)}) collective-permute-start(bf16[1,128,256]{2,1,0:T(8,128)(2,1)S(1)} %collective-permute-done.3), channel_id=1, source_target_pairs={{0,1},{1,2},{2,3},{3,4},{4,5},{5,6},{6,7},{7,8},{8,9},{9,10},{10,1... | collective-permute-start | bytes 196616 | tf_op jit(solution)/shard_map/ppermute | solution.py:21
  28.2 6.4 %collective-permute-start.5 = (bf16[1,128,256]{2,1,0:T(8,128)(2,1)S(1)}, bf16[1,128,256]{2,1,0:T(8,128)(2,1)S(1)}, u32[]{:S(2)}, u32[]{:S(2)}) collective-permute-start(bf16[1,128,256]{2,1,0:T(8,128)(2,1)S(1)} %collective-permute-done.4), channel_id=1, source_target_pairs={{0,1},{1,2},{2,3},{3,4},{4,5},{5,6},{6,7},{7,8},{8,9},{9,10},{10,1... | collective-permute-start | bytes 196616 | tf_op jit(solution)/shard_map/ppermute | solution.py:21
  33.9 12.9 %copy-start.2 = (bf16[1,128,1024]{2,1,0:T(8,128)(2,1)S(1)}, bf16[1,128,1024]{2,1,0:T(8,128)(2,1)}, u32[]{:S(2)}) copy-start(bf16[1,128,1024]{2,1,0:T(8,128)(2,1)} %param.8) | copy-start | bytes 786436
  33.9 36.5 %copy-start.1 = (bf16[1,128,256]{2,1,0:T(8,128)(2,1)S(1)}, bf16[1,128,256]{2,1,0:T(8,128)(2,1)}, u32[]{:S(2)}) copy-start(bf16[1,128,256]{2,1,0:T(8,128)(2,1)} %param.9) | copy-start | bytes 196612
  34.6 6.3 %copy-start.3 = (bf16[1,128,256]{2,1,0:T(8,128)(2,1)}, bf16[1,128,256]{2,1,0:T(8,128)(2,1)S(1)}, u32[]{:S(2)}) copy-start(bf16[1,128,256]{2,1,0:T(8,128)(2,1)S(1)} %collective-permute-done.5) | copy-start | bytes 196612
  34.6 12.4 %collective-permute-start.6 = (bf16[1,128,256]{2,1,0:T(8,128)(2,1)S(1)}, bf16[1,128,256]{2,1,0:T(8,128)(2,1)S(1)}, u32[]{:S(2)}, u32[]{:S(2)}) collective-permute-start(bf16[1,128,256]{2,1,0:T(8,128)(2,1)S(1)} %collective-permute-done.5), channel_id=1, source_target_pairs={{0,1},{1,2},{2,3},{3,4},{4,5},{5,6},{6,7},{7,8},{8,9},{9,10},{10,1... | collective-permute-start | bytes 196616 | tf_op jit(solution)/shard_map/ppermute | solution.py:21
  40.9 61.9 %copy-start.16 = (s32[2,2]{1,0:T(2,128)S(1)}, s32[2,2]{1,0:T(2,128)}, u32[]{:S(2)}) copy-start(s32[2,2]{1,0:T(2,128)} %param.13) | copy-start | bytes 52
  40.9 69.9 %copy-start.15 = (s32[2,16]{1,0:T(2,128)S(1)}, s32[2,16]{1,0:T(2,128)}, u32[]{:S(2)}) copy-start(s32[2,16]{1,0:T(2,128)} %param.11) | copy-start | bytes 388
  40.9 87.9 %all-to-all-start = ((bf16[16,128,256]{2,1,0:T(8,128)(2,1)}), bf16[16,128,256]{2,1,0:T(8,128)(2,1)S(1)}, u32[]{:S(2)}, u32[]{:S(2)}) async-start(bf16[16,128,256]{2,1,0:T(8,128)(2,1)} %fusion.22), calls=%async_computation | async-start | bytes 2097152 | tf_op jit(solution)/shard_map/all_to_all | solution.py:95
  46.8 66.8 %copy-start.17 = (s32[2]{0:T(128)S(1)}, s32[2]{0:T(128)}, u32[]{:S(2)}) copy-start(s32[2]{0:T(128)} %param.12) | copy-start | bytes 28
  47.0 67.8 %copy-start.5 = (bf16[1,128,256]{2,1,0:T(8,128)(2,1)}, bf16[1,128,256]{2,1,0:T(8,128)(2,1)S(1)}, u32[]{:S(2)}) copy-start(bf16[1,128,256]{2,1,0:T(8,128)(2,1)S(1)} %collective-permute-done.6) | copy-start | bytes 196612
  47.0 18.3 %collective-permute-start.7 = (bf16[1,128,256]{2,1,0:T(8,128)(2,1)S(1)}, bf16[1,128,256]{2,1,0:T(8,128)(2,1)S(1)}, u32[]{:S(2)}, u32[]{:S(2)}) collective-permute-start(bf16[1,128,256]{2,1,0:T(8,128)(2,1)S(1)} %collective-permute-done.6), channel_id=1, source_target_pairs={{0,1},{1,2},{2,3},{3,4},{4,5},{5,6},{6,7},{7,8},{8,9},{9,10},{10,1... | collective-permute-start | bytes 196616 | tf_op jit(solution)/shard_map/ppermute | solution.py:21
  65.3 49.5 %copy-start.7 = (bf16[1,128,256]{2,1,0:T(8,128)(2,1)}, bf16[1,128,256]{2,1,0:T(8,128)(2,1)S(1)}, u32[]{:S(2)}) copy-start(bf16[1,128,256]{2,1,0:T(8,128)(2,1)S(1)} %collective-permute-done.7) | copy-start | bytes 196612
  65.3 6.5 %collective-permute-start.8 = (bf16[1,128,256]{2,1,0:T(8,128)(2,1)S(1)}, bf16[1,128,256]{2,1,0:T(8,128)(2,1)S(1)}, u32[]{:S(2)}, u32[]{:S(2)}) collective-permute-start(bf16[1,128,256]{2,1,0:T(8,128)(2,1)S(1)} %collective-permute-done.7), channel_id=1, source_target_pairs={{0,1},{1,2},{2,3},{3,4},{4,5},{5,6},{6,7},{7,8},{8,9},{9,10},{10,1... | collective-permute-start | bytes 196616 | tf_op jit(solution)/shard_map/ppermute | solution.py:21
  71.8 43.0 %copy-start.9 = (bf16[1,128,256]{2,1,0:T(8,128)(2,1)}, bf16[1,128,256]{2,1,0:T(8,128)(2,1)S(1)}, u32[]{:S(2)}) copy-start(bf16[1,128,256]{2,1,0:T(8,128)(2,1)S(1)} %collective-permute-done.8) | copy-start | bytes 196612
  71.8 6.4 %collective-permute-start.9 = (bf16[1,128,256]{2,1,0:T(8,128)(2,1)S(1)}, bf16[1,128,256]{2,1,0:T(8,128)(2,1)S(1)}, u32[]{:S(2)}, u32[]{:S(2)}) collective-permute-start(bf16[1,128,256]{2,1,0:T(8,128)(2,1)S(1)} %collective-permute-done.8), channel_id=1, source_target_pairs={{0,1},{1,2},{2,3},{3,4},{4,5},{5,6},{6,7},{7,8},{8,9},{9,10},{10,1... | collective-permute-start | bytes 196616 | tf_op jit(solution)/shard_map/ppermute | solution.py:21
  78.2 17.9 %copy-start.11 = (bf16[1,128,256]{2,1,0:T(8,128)(2,1)}, bf16[1,128,256]{2,1,0:T(8,128)(2,1)S(1)}, u32[]{:S(2)}) copy-start(bf16[1,128,256]{2,1,0:T(8,128)(2,1)S(1)} %collective-permute-done.9) | copy-start | bytes 196612
  78.2 6.4 %collective-permute-start.10 = (bf16[1,128,256]{2,1,0:T(8,128)(2,1)S(1)}, bf16[1,128,256]{2,1,0:T(8,128)(2,1)S(1)}, u32[]{:S(2)}, u32[]{:S(2)}) collective-permute-start(bf16[1,128,256]{2,1,0:T(8,128)(2,1)S(1)} %collective-permute-done.9), channel_id=1, source_target_pairs={{0,1},{1,2},{2,3},{3,4},{4,5},{5,6},{6,7},{7,8},{8,9},{9,10},{10,1... | collective-permute-start | bytes 196616 | tf_op jit(solution)/shard_map/ppermute | solution.py:21
  84.6 11.6 %copy-start.13 = (bf16[1,128,256]{2,1,0:T(8,128)(2,1)}, bf16[1,128,256]{2,1,0:T(8,128)(2,1)S(1)}, u32[]{:S(2)}) copy-start(bf16[1,128,256]{2,1,0:T(8,128)(2,1)S(1)} %collective-permute-done.10) | copy-start | bytes 196612
  84.6 6.4 %collective-permute-start.11 = (bf16[1,128,256]{2,1,0:T(8,128)(2,1)S(1)}, bf16[1,128,256]{2,1,0:T(8,128)(2,1)}, u32[]{:S(2)}, u32[]{:S(2)}) collective-permute-start(bf16[1,128,256]{2,1,0:T(8,128)(2,1)S(1)} %collective-permute-done.10), channel_id=1, source_target_pairs={{0,1},{1,2},{2,3},{3,4},{4,5},{5,6},{6,7},{7,8},{8,9},{9,10},{10,1... | collective-permute-start | bytes 196616 | tf_op jit(solution)/shard_map/ppermute | solution.py:21
  91.0 6.8 %collective-permute-start.12 = (bf16[1,128,256]{2,1,0:T(8,128)(2,1)}, bf16[1,128,256]{2,1,0:T(8,128)(2,1)}, u32[]{:S(2)}, u32[]{:S(2)}) collective-permute-start(bf16[1,128,256]{2,1,0:T(8,128)(2,1)} %collective-permute-done.11), channel_id=1, source_target_pairs={{0,1},{1,2},{2,3},{3,4},{4,5},{5,6},{6,7},{7,8},{8,9},{9,10},{10,1... | collective-permute-start | bytes 196616 | tf_op jit(solution)/shard_map/ppermute | solution.py:21
  97.8 6.7 %collective-permute-start.13 = (bf16[1,128,256]{2,1,0:T(8,128)(2,1)}, bf16[1,128,256]{2,1,0:T(8,128)(2,1)}, u32[]{:S(2)}, u32[]{:S(2)}) collective-permute-start(bf16[1,128,256]{2,1,0:T(8,128)(2,1)} %collective-permute-done.12), channel_id=1, source_target_pairs={{0,1},{1,2},{2,3},{3,4},{4,5},{5,6},{6,7},{7,8},{8,9},{9,10},{10,1... | collective-permute-start | bytes 196616 | tf_op jit(solution)/shard_map/ppermute | solution.py:21
  104.5 10.7 %collective-permute-start.14 = (bf16[1,128,256]{2,1,0:T(8,128)(2,1)}, bf16[1,128,256]{2,1,0:T(8,128)(2,1)}, u32[]{:S(2)}, u32[]{:S(2)}) collective-permute-start(bf16[1,128,256]{2,1,0:T(8,128)(2,1)} %collective-permute-done.13), channel_id=1, source_target_pairs={{0,1},{1,2},{2,3},{3,4},{4,5},{5,6},{6,7},{7,8},{8,9},{9,10},{10,1... | collective-permute-start | bytes 196616 | tf_op jit(solution)/shard_map/ppermute | solution.py:21
  115.1 12.1 %copy-start.10 = (bf16[1,128,256]{2,1,0:T(8,128)(2,1)S(1)}, bf16[1,128,256]{2,1,0:T(8,128)(2,1)}, u32[]{:S(2)}) copy-start(bf16[1,128,256]{2,1,0:T(8,128)(2,1)} %copy-done.9) | copy-start | bytes 196612
  115.1 12.2 %copy-start.8 = (bf16[1,128,256]{2,1,0:T(8,128)(2,1)S(1)}, bf16[1,128,256]{2,1,0:T(8,128)(2,1)}, u32[]{:S(2)}) copy-start(bf16[1,128,256]{2,1,0:T(8,128)(2,1)} %copy-done.7) | copy-start | bytes 196612
  115.1 12.2 %copy-start.6 = (bf16[1,128,256]{2,1,0:T(8,128)(2,1)S(1)}, bf16[1,128,256]{2,1,0:T(8,128)(2,1)}, u32[]{:S(2)}) copy-start(bf16[1,128,256]{2,1,0:T(8,128)(2,1)} %copy-done.5) | copy-start | bytes 196612
  115.1 12.2 %copy-start.4 = (bf16[1,128,256]{2,1,0:T(8,128)(2,1)S(1)}, bf16[1,128,256]{2,1,0:T(8,128)(2,1)}, u32[]{:S(2)}) copy-start(bf16[1,128,256]{2,1,0:T(8,128)(2,1)} %copy-done.3) | copy-start | bytes 196612
  115.2 12.0 %copy-start.14 = (bf16[1,128,256]{2,1,0:T(8,128)(2,1)S(1)}, bf16[1,128,256]{2,1,0:T(8,128)(2,1)}, u32[]{:S(2)}) copy-start(bf16[1,128,256]{2,1,0:T(8,128)(2,1)} %copy-done.13) | copy-start | bytes 196612
  115.2 12.0 %copy-start.12 = (bf16[1,128,256]{2,1,0:T(8,128)(2,1)S(1)}, bf16[1,128,256]{2,1,0:T(8,128)(2,1)}, u32[]{:S(2)}) copy-start(bf16[1,128,256]{2,1,0:T(8,128)(2,1)} %copy-done.11) | copy-start | bytes 196612
